TPU v7x, 128 devices: a whole 4x4x4 slice. The times are simulated.
128 devices in a mesh: doc: 8 (over x, core), term: 16 (over z, y).
Axes of the slice: x: 4, y: 4, z: 4, core: 2. Of those that a mesh axis runs over, the one named last changes fastest.
Arguments:
- query_states: bfloat16 [512, 32, 768], P('doc'), may hold values from -6 to 6
- token_ids: int32 [512, 32], P('doc'), may hold values from 0 to 30521, as said below
- transform_weight: bfloat16 [768, 768], replicated, may hold values from -0.21875 to 0.21875
- transform_bias: float32 [768], replicated, may hold values from -3 to 3
- norm_gain: float32 [768], replicated, may hold values from 0.5 to 1.5
- norm_bias: float32 [768], replicated, may hold values from -3 to 3
- decoder_weight: bfloat16 [768, 30720], P(None, 'term'), may hold values from -0.21875 to 0.21875
- decoder_bias: float32 [30720], P('term'), may hold values from -2.5 to 0.5
- candidates: int32 [512, 32], P('doc'), may hold values from 0 to 127, all different within a row; in each aligned block of 64 rows (0 to 63, 64 to 127, ...) at most 32 rows name the same one
- occupancy: int32 [128, 240], P('doc', 'term'), may hold values 0 or 1
- doc_blocks: bfloat16 [128, 240, 128, 128], P('doc', 'term'), may hold values from -0.046875 to 0.046875
Outputs:
- query_weights: bfloat16 [512, 30720], P('doc', 'term')
- scores: float32 [512, 32, 128], P('doc', None, 'term')
Inputs may be any that keep to these rules, and one draw needn't show every extreme that they name: `token_ids`: id 0 marks padding: a query has non-zero ids at its first positions, at least 8 of them, and 0 after them. `candidates`: A query names 32 different tiles; among the 64 queries of one doc index no tile is named by more than 32 of them.
All inputs are finite; a program needn't handle non-finite values. No bound on the sum of `occupancy` on one device may be relied on, other than what follows from the above.
Results may differ from a plain program's by a relative error of at most 0.0041.
Values may be sent and summed in bfloat16 or wider, within the bound.
A program may use at most 128 MiB of HBM per device.

v0:
```python
import jax
import jax.numpy as jnp
from jax import lax
from jax.sharding import PartitionSpec as P

VOCAB = 30522
MOST = 32


def tile_ranks(cand_rows, tile_total):
    tile_index = lax.iota(jnp.int32, tile_total)
    tile_hits = jnp.sum((cand_rows[..., None] == tile_index).astype(jnp.int32), axis=-2)
    tile_before = jnp.cumsum(tile_hits, axis=-2) - tile_hits
    return (tile_hits, tile_before)


def slot_sources(hits_by_tile, before_by_tile, capacity):
    row_total = hits_by_tile.shape[-1]
    slot_index = lax.iota(jnp.int32, capacity)
    chosen = (hits_by_tile[..., None, :] > 0) & (
        before_by_tile[..., None, :] == slot_index[:, None]
    )
    source_row = jnp.sum(jnp.where(chosen, lax.iota(jnp.int32, row_total), 0), axis=-1)
    return (source_row, jnp.any(chosen, axis=-1))


def body(
    query_states,
    token_ids,
    transform_weight,
    transform_bias,
    norm_gain,
    norm_bias,
    decoder_weight,
    decoder_bias,
    candidates,
    occupancy,
    doc_blocks,
):
    query_count, query_length, model_width = query_states.shape
    vocab_local = decoder_weight.shape[1]
    tile_local, blocks_local, tile_docs, block_terms = doc_blocks.shape
    cand_count = candidates.shape[1]
    term_index = lax.axis_index("term")
    doc_index = lax.axis_index("doc")
    doc_count = lax.axis_size("doc")
    term_count = lax.axis_size("term")
    tile_total = doc_count * tile_local
    hidden = (
        jnp.dot(
            query_states.reshape(query_count * query_length, model_width),
            transform_weight,
            preferred_element_type=jnp.float32,
        )
        + transform_bias
    )
    hidden = jax.nn.gelu(hidden, approximate=False)
    centred = hidden - jnp.mean(hidden, axis=-1, keepdims=True)
    spread = jnp.mean(centred * centred, axis=-1, keepdims=True)
    normed = (centred * lax.rsqrt(spread + 1e-06) * norm_gain + norm_bias).astype(jnp.bfloat16)
    logits = jnp.dot(normed, decoder_weight, preferred_element_type=jnp.float32) + decoder_bias
    activated = jnp.log1p(jnp.maximum(logits, 0.0)).reshape(query_count, query_length, vocab_local)
    live_mask = (token_ids != 0).astype(jnp.float32)[:, :, None]
    columns = term_index * vocab_local + lax.iota(jnp.int32, vocab_local)
    vocab_keep = (columns < VOCAB).astype(jnp.float32)
    weights = (jnp.max(activated * live_mask, axis=1) * vocab_keep).astype(jnp.bfloat16)
    own_hits, own_before = tile_ranks(candidates, tile_total)
    all_weights, all_cand = (
        lax.all_gather(weights, "doc", axis=0, tiled=True),
        lax.all_gather(candidates, "doc", axis=0, tiled=True),
    )
    local_cand = (all_cand - doc_index * tile_local).reshape(doc_count, query_count, cand_count)
    tile_hits, tile_before = tile_ranks(local_cand, tile_local)
    source_row, slot_valid = slot_sources(
        jnp.swapaxes(tile_hits, 1, 2), jnp.swapaxes(tile_before, 1, 2), MOST
    )
    flat_index = lax.iota(jnp.int32, doc_count)[:, None, None] * query_count + source_row
    buffer = jnp.take(all_weights, flat_index.reshape(-1), axis=0).reshape(
        doc_count, tile_local, MOST, vocab_local
    )
    buffer = buffer * slot_valid.astype(jnp.bfloat16)[..., None]
    occupied = occupancy.astype(jnp.bfloat16)
    masked = (
        buffer.reshape(doc_count, tile_local, MOST, blocks_local, block_terms)
        * occupied[None, :, None, :, None]
    )
    partial_value = jnp.einsum(
        "jtrbc,tbdc->jtrd", masked, doc_blocks, preferred_element_type=jnp.float32
    )
    slice_width = tile_docs // term_count
    score_total = lax.psum(partial_value, "term")
    score_share = lax.dynamic_slice_in_dim(score_total, term_index * slice_width, slice_width, 3)
    returned = lax.all_to_all(score_share, "doc", split_axis=0, concat_axis=1, tiled=True)
    slot_rank = jnp.take_along_axis(own_before, candidates, axis=1)
    flat_index = candidates * MOST + slot_rank
    scores = jnp.take(returned.reshape(-1, slice_width), flat_index.reshape(-1), axis=0)
    scores = scores.reshape(query_count, cand_count, slice_width)
    return (weights, scores)


def solution(mesh):
    placed = (
        P("doc", None, None),
        P("doc", None),
        P(),
        P(),
        P(),
        P(),
        P(None, "term"),
        P("term"),
        P("doc", None),
        P("doc", "term"),
        P("doc", "term", None, None),
    )
    return jax.shard_map(
        body,
        mesh=mesh,
        in_specs=placed,
        out_specs=(P("doc", "term"), P("doc", None, "term")),
        check_vma=False,
    )
```

profile of v0, /device:TPU:1, one launch (start us, length us, event | category | flops | bytes accessed | tf_op | source)
XLA Modules:
  0.0 286.4 jit_solution(9171432627118115750)
XLA Ops:
  7.2 0.9 copy.49
  9.1 17.5 %fusion.25 = (f32[2048]{0:T(1024)S(1)}, f32[2048,768]{0,1:T(8,128)S(1)}) fusion(f32[768]{0:T(1024)} %param.14, bf16[2048,768]{1,0:T(8,128)(2,1)S(1)} %bitcast.34, bf16[768,768]{1,0:T(8,128)(2,1)} %param.13), kind=kOutput, calls=%fused_computation.67 | convolution fusion | flops 2519726080 | bytes 10628096 | tf_op jit(solution)/shard_map/dot_general | solution.py:50
  27.4 1.1 copy-done.4
  28.5 13.7 %multiply_reduce_fusion = f32[64,1920]{1,0:T(8,128)S(1)} fusion(f32[64,32]{1,0:T(8,128)S(1)} %compare_convert_fusion, f32[1920]{0:T(1024)S(1)} %copy-done.5, bf16[768,1920]{1,0:T(8,128)(2,1)S(1)} %copy-done.4, f32[2048,768]{0,1:T(8,128)S(1)} %get-tuple-element.7, f32[768]{0:T(1024)S(1)} %copy-done.6, f32[768]{0:T(1024)S(1)} %copy-done.7, ...), kind=kOutput, calls=%fused_computation.6 | convolution fusion | flops 6063267840 | bytes 9770496 | tf_op jit(solution)/shard_map/dot_general | solution.py:61
  43.0 14.4 %all-gather = s32[8,64,32]{1,2,0:T(8,128)S(1)} all-gather(s32[1,64,32]{1,2,0:T(8,128)S(1)} %bitcast.39), channel_id=1, replica_groups=mesh['doc'=8,'term'=16] {'doc'}, dimensions={0}, use_global_device_ids=true | all-gather | bytes 73728 | tf_op jit(solution)/shard_map/all_gather | solution.py:70
  57.9 6.6 %fusion.23 = s32[8,16,64]{1,0,2:T(8,128)S(1)} fusion(s32[8,64,16]{2,0,1:T(8,128)S(1)} %copy.56), kind=kOutput, calls=%fused_computation.43 | output fusion | flops 524288 | bytes 65536 | tf_op jit(solution)/shard_map/jit(cumsum)/reduce_window_sum | solution.py:13
  64.6 2.2 select_reduce_fusion
  67.1 2.3 fusion.17
  69.4 2.2 all-gather.3.cloned.1.call-done
  71.6 31.8 %gather_fusion = bf16[4096,1920]{1,0:T(8,128)(2,1)} fusion(bf16[512,1920]{1,0:T(8,128)(2,1)} %all-gather.3.cloned.1.call-done, s32[4096]{0:T(1024)S(1)} %broadcast_clamp_fusion), kind=kCustom, calls=%fused_computation | custom fusion | bytes 31473664 | tf_op jit(solution)/shard_map/jit(_take)/gather | solution.py:78
  103.4 27.2 %gather.18 = bf16[8,16,32,15,128]{4,3,2,1,0:T(8,128)(2,1)} reshape(bf16[4096,1920]{1,0:T(8,128)(2,1)} %gather_fusion) | data formatting | bytes 31457280 | tf_op jit(solution)/shard_map/jit(_take)/gather | solution.py:78
  130.6 14.0 %multiply_multiply_fusion = bf16[8,16,32,15,128]{4,3,2,1,0:T(8,128)(2,1)} fusion(bf16[8,16,32,15,128]{4,3,2,1,0:T(8,128)(2,1)} %gather.18, pred[8,16,32]{2,1,0:T(8,128)(4,1)S(1)} %get-tuple-element.4, bf16[16,15]{1,0:T(8,128)(2,1)S(1)} %convert_element_type.39, bf16[8,16,32]{2,1,0:T(8,128)(2,1)S(1)} %convert_element_type.38), kind=kLoop, calls=%fused_computation.3 | loop fusion | flops 23592960 | bytes 31470048 | tf_op jit(solution)/shard_map/mul | solution.py:84
  144.6 13.5 %fusion.18 = f32[8,16,32,128]{3,2,0,1:T(8,128)} fusion(bf16[16,15,128,128]{3,2,1,0:T(8,128)(2,1)} %param.21, bf16[8,16,32,15,128]{4,3,2,1,0:T(8,128)(2,1)} %multiply_multiply_fusion), kind=kOutput, calls=%fused_computation.39 | convolution fusion | flops 2013265920 | bytes 25690112 | tf_op jit(solution)/shard_map/jtrbc,tbdc->jtrd/dot_general | solution.py:87
  158.8 13.1 %gather_fusion.2 = s32[2048]{0:T(1024)S(1)} fusion(s32[64,128]{1,0:T(8,128)S(1)} %sub.26, s32[2048]{0:T(1024)S(1)} %reshape.174), kind=kCustom, calls=%fused_computation.2 | custom fusion | bytes 32768 | tf_op jit(solution)/shard_map/jit(take_along_axis)/gather | solution.py:94
  172.1 75.3 %all-reduce.2.cloned.1.call-done = f32[8,16,32,128]{3,2,0,1:T(8,128)} async-done(((f32[8,16,32,128]{3,2,0,1:T(8,128)}), f32[8,16,32,128]{3,2,0,1:T(8,128)}) %all-reduce.2.cloned.1.call-update) | async-done | bytes 2097168 | tf_op jit(solution)/shard_map/psum | solution.py:91
  247.4 2.2 constant_dynamic-slice_fusion
  250.2 0.9 reshape.192
  251.2 6.0 %all-to-all-start = ((f32[8,1,4096]{2,1,0:T(1,128)}), f32[8,1,4096]{2,1,0:T(1,128)S(1)}, u32[]{:S(2)}, u32[]{:S(2)}) async-start(f32[8,1,4096]{2,1,0:T(1,128)} %reshape.192), calls=%async_computation | async-start | bytes 262144 | tf_op jit(solution)/shard_map/all_to_all | solution.py:93
  257.1 5.3 %all-to-all-done = f32[8,1,4096]{2,1,0:T(1,128)S(1)} async-done(((f32[8,1,4096]{2,1,0:T(1,128)}), f32[8,1,4096]{2,1,0:T(1,128)S(1)}, u32[]{:S(2)}, u32[]{:S(2)}) %all-to-all-start) | async-done | bytes 131104 | tf_op jit(solution)/shard_map/all_to_all | solution.py:93
  262.9 1.0 reduce
  263.9 1.0 reshape.193
  264.8 3.2 %copy.66 = f32[8,16,32,8]{3,2,1,0:T(8,128)} copy(f32[8,16,32,8]{2,3,1,0:T(8,128)} %bitcast.38) | data formatting | bytes 262144 | tf_op jit(solution)/shard_map/reshape | solution.py:96
  268.0 9.1 %gather_fusion.1 = f32[2048,8]{1,0:T(8,128)} fusion(f32[4096,8]{1,0:T(8,128)} %bitcast.35, s32[2048]{0:T(1024)S(1)} %broadcast_clamp_fusion.1), kind=kCustom, calls=%fused_computation.1 | custom fusion | bytes 139264 | tf_op jit(solution)/shard_map/jit(_take)/gather | solution.py:96
  277.2 1.8 copy.63
  (52 shorter events, 6.0 us)
Async XLA Ops:
  7.2 1.9 copy-start
  7.2 64.4 %all-gather.3.cloned.1.call-start = ((), (), s32[]{:S(2)}) async-start(), calls=%async_computation.1 | async-start | bytes 2211840 | tf_op jit(solution)/shard_map/all_gather | solution.py:69
  26.6 1.8 copy-start.4
  26.6 1.8 copy-start.5
  26.6 1.8 copy-start.6
  26.6 1.8 copy-start.7
  28.4 14.5 %copy-start.3 = (s32[16,15]{1,0:T(8,128)S(1)}, s32[16,15]{1,0:T(8,128)}, u32[]{:S(2)}) copy-start(s32[16,15]{1,0:T(8,128)} %param.20) | copy-start | bytes 2884
  28.4 14.6 %copy-start.2 = (s32[64,32]{0,1:T(8,128)S(1)}, s32[64,32]{0,1:T(8,128)}, u32[]{:S(2)}) copy-start(s32[64,32]{0,1:T(8,128)} %param.19) | copy-start | bytes 24580
  42.9 204.5 %all-reduce.2.cloned.1.call-start = ((), (), s32[]{:S(2)}) async-start(), calls=%async_computation.2 | async-start | bytes 4194304 | tf_op jit(solution)/shard_map/psum | solution.py:91
  251.2 11.2 %all-to-all-start = ((f32[8,1,4096]{2,1,0:T(1,128)}), f32[8,1,4096]{2,1,0:T(1,128)S(1)}, u32[]{:S(2)}, u32[]{:S(2)}) async-start(f32[8,1,4096]{2,1,0:T(1,128)} %reshape.192), calls=%async_computation | async-start | bytes 262144 | tf_op jit(solution)/shard_map/all_to_all | solution.py:93
  264.8 14.8 %copy-start.1 = (bf16[64,32,768]{2,1,0:T(8,128)(2,1)S(1)}, bf16[64,32,768]{2,1,0:T(8,128)(2,1)}, u32[]{:S(2)}) copy-start(bf16[64,32,768]{2,1,0:T(8,128)(2,1)} %param.11) | copy-start | bytes 9437188
Sparse Core Ops, SparseCore 0:
  43.0 28.5 all-gather.2
  158.2 89.1 all-reduce.1
where the time goes:
time: 288 us; the launch traced here: 286 us
  local copies, waits for them, and re-layouts  95 us (33%)
  waiting for transfers between devices  82.8 us (29%)
  matrix products  44.7 us (16%)
  other arithmetic  29.1 us (10%)
  blocking collectives  14.4 us (5%)
  between operations  14.3 us (5%)
  starting transfers between devices  6.05 us (2%)
    psum x1, waiting for transfers between devices, body(): score_total = lax.psum(partial_value, 'term')  75.3 us
    gather x2, local copies, waits for them, and re-layouts, body(): jnp.take(all_weights, flat_index.reshape(-1), axis=0)  59 us
    dot_general x1, matrix products, body(): jnp.dot(query_states.reshape(query_count * query_length, model_width), tr...  17.5 us
    all_gather x1, blocking collectives, body(): lax.all_gather(candidates, 'doc', axis=0, tiled=True)  14.4 us
    mul x1, other arithmetic, body(): buffer.reshape(doc_count, tile_local, MOST, blocks_local, block_terms)  14 us
    dot_general x1, matrix products, body(): jnp.dot(normed, decoder_weight, preferred_element_type=jnp.float32)  13.7 us
    dot_general x1, matrix products, body(): jnp.einsum('jtrbc,tbdc->jtrd', masked, doc_blocks, preferred_element_type...  13.5 us
    gather x3, local copies, waits for them, and re-layouts, body(): slot_rank = jnp.take_along_axis(own_before, candidates, axis=1)  13.2 us
  transfers between devices with their start and end apart: 3, of which 3 were waited for; matrix products, arithmetic and copies ran while one was open for 9% of the time, Pallas kernels for 0%

commit v1 on v0

v1 whole, which is shorter than its diff:
```python
import jax
import jax.numpy as jnp
from jax import lax
from jax.experimental import pallas as pl
from jax.experimental.pallas import tpu as pltpu
from jax.sharding import PartitionSpec as P

MESH = pl.DeviceIdType.MESH
VOCAB = 30522
NDOC = 8
NY = 4
NZ = 4
QD = 64
QLEN = 32
DM = 768
VL = 1920
NB = 15
NTL = 16
CAND = 32
CH = 16
TOK = CH * QLEN
HQ = 32
HL = NDOC * HQ
COLS = 384
BF = jnp.bfloat16
F32 = jnp.float32


def kernel(
    x_hbm, tok_ref, tw_hbm, tb_ref, g_ref, nb_ref, dw_hbm, db_ref, cand_ref, occ_ref, docs_hbm,
    qw_ref, out_ref,
    xv, twv, dwv, dv, occrow, lens, nrm, wall, wt, sbuf, rbuf, s2buf, r2buf, pbuf, back,
    xsem, wsem, dsem, ag_s, ag_r, s1_s, s1_r, s2_s, s2_r, rt_s, rt_r,
):
    doc = lax.axis_index("doc")
    term = lax.axis_index("term")
    z = term // NY
    y = lax.rem(term, NY)

    tw_cp = pltpu.make_async_copy(tw_hbm, twv, wsem.at[0])
    tw_cp.start()
    dw_cp = pltpu.make_async_copy(dw_hbm, dwv, wsem.at[1])

    def x_copy(c):
        return pltpu.make_async_copy(x_hbm.at[pl.ds(c * CH, CH)], xv.at[pl.ds(c * CH, CH)], xsem.at[c])

    def d_copy(b):
        return pltpu.make_async_copy(docs_hbm.at[:, b], dv.at[:, :, pl.ds(b * 128, 128)], dsem.at[b])

    x_copy(0).start()
    dw_cp.start()
    for c in range(1, 4):
        x_copy(c).start()
    for b in range(NB):
        d_copy(b).start()

    barrier = pltpu.get_barrier_semaphore()
    for k in range(1, NDOC):
        pl.semaphore_signal(barrier, inc=1, device_id={"doc": lax.rem(doc + k, NDOC)}, device_id_type=MESH)
    for k in range(1, 4):
        pl.semaphore_signal(barrier, inc=1, device_id={"term": z * NY + lax.rem(y + k, NY)}, device_id_type=MESH)
        pl.semaphore_signal(barrier, inc=1, device_id={"term": lax.rem(z + k, NZ) * NY + y}, device_id_type=MESH)

    live = jnp.where(tok_ref[...] != 0, 1.0, 0.0).astype(BF)
    lens[...] = lax.dot_general(
        live, jnp.ones((QLEN, DM), BF), (((0,), (0,)), ((), ())), preferred_element_type=F32
    )
    spread = jnp.where(
        lax.broadcasted_iota(jnp.int32, (NB, VL), 1) // 128 == lax.broadcasted_iota(jnp.int32, (NB, VL), 0), 1.0, 0.0
    ).astype(BF)
    occrow[...] = jnp.dot(occ_ref[...].astype(F32).astype(BF), spread, preferred_element_type=F32)

    def ag_copy(c, k):
        half, sub = c // 2, lax.rem(c, 2)
        place = wall.at[half, doc, pl.ds(sub * CH, CH)]
        return pltpu.make_async_remote_copy(
            src_ref=place, dst_ref=place, send_sem=ag_s.at[c, k], recv_sem=ag_r.at[c, k],
            device_id={"doc": lax.rem(doc + k + 1, NDOC)}, device_id_type=MESH,
        )

    def expand(c):
        x_copy(c).wait()
        rows = pl.ds(pl.multiple_of(c * CH, CH), CH)
        h = jnp.dot(xv[rows].reshape(TOK, DM), twv[...], preferred_element_type=F32) + tb_ref[...]
        h = 0.5 * h * (1.0 + lax.erf(h * 0.7071067811865476))
        cen = h - jnp.mean(h, axis=-1, keepdims=True)
        var = jnp.mean(cen * cen, axis=-1, keepdims=True)
        n = cen * lax.rsqrt(var + 1e-6) * g_ref[...] + nb_ref[...]
        n3 = n.reshape(CH, QLEN, DM)
        pos = lax.broadcasted_iota(jnp.int32, (CH, QLEN, DM), 1).astype(F32)
        n3 = jnp.where(pos < lens[rows, :][:, None, :], n3, n3[:, 0:1, :])
        nrm[...] = n3.reshape(TOK, DM).astype(BF)

    def decode(c):
        half, sub = c // 2, lax.rem(c, 2)
        rows = pl.ds(pl.multiple_of(c * CH, CH), CH)
        srow = pl.ds(pl.multiple_of(sub * CH, CH), CH)
        for c0 in range(0, VL, COLS):
            lg = jnp.dot(nrm[...], dwv[:, c0:c0 + COLS], preferred_element_type=F32)
            top = jnp.max(lg.reshape(CH, QLEN, COLS), axis=1) + db_ref[:, c0:c0 + COLS]
            w = jnp.log1p(jnp.maximum(top, 0.0))
            col = term * VL + c0 + lax.broadcasted_iota(jnp.int32, (CH, COLS), 1)
            w = jnp.where(col < VOCAB, w, 0.0).astype(BF)
            wall[half, doc, srow, c0:c0 + COLS] = w
            qw_ref[rows, c0:c0 + COLS] = w

    def ag_start(c):
        for k in range(NDOC - 1):
            ag_copy(c, k).start()

    def ag_wait(c):
        for k in range(NDOC - 1):
            ag_copy(c, k).wait_recv()

    def s1_copy(half, g, k, y_first):
        if y_first:
            peer = lax.rem(y + k + 1, NY)
            to = {"term": z * NY + peer}
        else:
            peer = lax.rem(z + k + 1, NZ)
            to = {"term": peer * NY + y}
        return pltpu.make_async_remote_copy(
            src_ref=sbuf.at[half, g, peer], dst_ref=rbuf.at[half, g, k],
            send_sem=s1_s.at[half, g, k], recv_sem=s1_r.at[half, g, k], device_id=to, device_id_type=MESH,
        )

    def s2_copy(half, g, k, y_first):
        if y_first:
            peer = lax.rem(z + k + 1, NZ)
            to = {"term": peer * NY + y}
        else:
            peer = lax.rem(y + k + 1, NY)
            to = {"term": z * NY + peer}
        return pltpu.make_async_remote_copy(
            src_ref=s2buf.at[half, g, peer], dst_ref=r2buf.at[half, g, k],
            send_sem=s2_s.at[half, g, k], recv_sem=s2_r.at[half, g, k], device_id=to, device_id_type=MESH,
        )

    def rt_copy(half, k):
        peer = lax.rem(doc + k + 1, NDOC)
        return pltpu.make_async_remote_copy(
            src_ref=pbuf.at[half, peer], dst_ref=back.at[half, doc],
            send_sem=rt_s.at[half, k], recv_sem=rt_r.at[half, k], device_id={"doc": peer}, device_id_type=MESH,
        )

    def mask_docs(g):
        for t in range(4):
            tile = g * 4 + t
            row = occrow[pl.ds(tile, 1), :].astype(BF)
            dv[tile] = dv[tile] * row

    def score(half):
        for c0 in range(0, VL, 128):
            part = wall[half, :, :, c0:c0 + 128].reshape(HL, 128)
            wt[c0:c0 + 128, :] = part.T

        for y_first in (True, False):
            @pl.loop(0, 2)
            def _(i):
                g = i if y_first else i + 2
                if half == 0:
                    mask_docs(g)
                docs = dv[pl.ds(g * 4, 4)].reshape(512, VL)
                r = jnp.dot(docs, wt[...], preferred_element_type=F32).reshape(4, NZ, NY, 8, HL)
                for zz in range(NZ):
                    for yy in range(NY):
                        part = jnp.concatenate([r[t, zz, yy] for t in range(4)], axis=0).astype(BF)
                        slot, at = (yy, zz) if y_first else (zz, yy)
                        sbuf[half, g, slot, at * 32:(at + 1) * 32, :] = part
                for k in range(3):
                    s1_copy(half, g, k, y_first).start()

    def reduce1(half):
        for g in range(4):
            y_first = g < 2
            for k in range(3):
                s1_copy(half, g, k, y_first).wait_recv()
            tot = sbuf[half, g, y if y_first else z].astype(F32)
            for k in range(3):
                tot = tot + rbuf[half, g, k].astype(F32)
            s2buf[half, g] = tot.astype(BF).reshape(4, 32, HL)
            for k in range(3):
                s2_copy(half, g, k, y_first).start()

    def reduce2(half):
        lane_group = lax.broadcasted_iota(jnp.int32, (8, 128), 1) // HQ
        for g in range(4):
            y_first = g < 2
            for k in range(3):
                s2_copy(half, g, k, y_first).wait_recv()
            tot = s2buf[half, g, z if y_first else y].astype(F32)
            for k in range(3):
                tot = tot + r2buf[half, g, k].astype(F32)
            for j in range(NDOC):
                made = jnp.zeros((8, 128), F32)
                for t in range(4):
                    piece = tot[t * 8:(t + 1) * 8, (j // 4) * 128:(j // 4 + 1) * 128]
                    turn = ((t - j % 4) * HQ) % 128
                    if turn:
                        piece = pltpu.roll(piece, turn, 1)
                    made = jnp.where(lane_group == t, piece, made)
                pbuf[half, j, g] = made
        for k in range(NDOC - 1):
            rt_copy(half, k).start()
        back[half, doc] = pbuf[half, doc]

    def select(half):
        for k in range(NDOC - 1):
            rt_copy(half, k).wait_recv()
        part = lax.broadcasted_iota(jnp.int32, (8, 128), 1) // HQ
        for c in range(CAND):
            row = cand_ref[half, c:c + 1, :]
            want = jnp.broadcast_to(row, (8, 128)) - part
            acc = jnp.zeros((8, 128), F32)
            for d in range(NDOC):
                for g in range(4):
                    acc = jnp.where(want == d * 16 + g * 4, back[half, d, g], acc)
            acc = acc + pltpu.roll(acc, 64, 1)
            acc = acc + pltpu.roll(acc, 32, 1)
            out_ref[c, :, half * HQ:(half + 1) * HQ] = acc[:, 0:HQ]

    tw_cp.wait()
    expand(0)
    dw_cp.wait()
    decode(0)
    pl.semaphore_wait(barrier, NDOC - 1 + 6)
    ag_start(0)

    @pl.loop(1, 3)
    def _(c):
        expand(c)
        decode(c)
        ag_start(c)

    for b in range(NB):
        d_copy(b).wait()
    ag_wait(0)
    ag_wait(1)
    score(0)
    expand(3)
    decode(3)
    ag_start(3)
    reduce1(0)
    ag_wait(2)
    ag_wait(3)
    score(1)
    reduce2(0)
    reduce1(1)
    select(0)
    reduce2(1)
    select(1)

    for c in range(4):
        for k in range(NDOC - 1):
            ag_copy(c, k).wait_send()
    for half in range(2):
        for g in range(4):
            for k in range(3):
                s1_copy(half, g, k, g < 2).wait_send()
                s2_copy(half, g, k, g < 2).wait_send()
        for k in range(NDOC - 1):
            rt_copy(half, k).wait_send()


def body(
    query_states, token_ids, transform_weight, transform_bias, norm_gain, norm_bias,
    decoder_weight, decoder_bias, candidates, occupancy, doc_blocks,
):
    cand = candidates.T.reshape(CAND, 2, 1, HQ)
    cand = jnp.broadcast_to(cand, (CAND, 2, 4, HQ)).transpose(1, 0, 2, 3).reshape(2, CAND, 128)
    any_ = pl.BlockSpec(memory_space=pl.ANY)
    vm = pl.BlockSpec(memory_space=pltpu.VMEM)
    dma = pltpu.SemaphoreType.DMA
    weights, picked = pl.pallas_call(
        kernel,
        out_shape=(
            jax.ShapeDtypeStruct((QD, VL), BF),
            jax.ShapeDtypeStruct((CAND, 8, QD), F32),
        ),
        in_specs=[any_, vm, any_, vm, vm, vm, any_, vm, vm, vm, any_],
        out_specs=(vm, vm),
        scratch_shapes=[
            pltpu.VMEM((QD, QLEN, DM), BF),
            pltpu.VMEM((DM, DM), BF),
            pltpu.VMEM((DM, VL), BF),
            pltpu.VMEM((NTL, 128, VL), BF),
            pltpu.VMEM((NTL, VL), F32),
            pltpu.VMEM((QD, DM), F32),
            pltpu.VMEM((TOK, DM), BF),
            pltpu.VMEM((2, NDOC, HQ, VL), BF),
            pltpu.VMEM((VL, HL), BF),
            pltpu.VMEM((2, 4, 4, 128, HL), BF),
            pltpu.VMEM((2, 4, 3, 128, HL), BF),
            pltpu.VMEM((2, 4, 4, 32, HL), BF),
            pltpu.VMEM((2, 4, 3, 32, HL), BF),
            pltpu.VMEM((2, NDOC, 4, 8, 128), F32),
            pltpu.VMEM((2, NDOC, 4, 8, 128), F32),
            dma((4,)),
            dma((2,)),
            dma((NB,)),
            dma((4, NDOC - 1)),
            dma((4, NDOC - 1)),
            dma((2, 4, 3)),
            dma((2, 4, 3)),
            dma((2, 4, 3)),
            dma((2, 4, 3)),
            dma((2, NDOC - 1)),
            dma((2, NDOC - 1)),
        ],
        compiler_params=pltpu.CompilerParams(
            collective_id=0, has_side_effects=True, vmem_limit_bytes=56 * 1024 * 1024
        ),
        name="splade",
    )(
        query_states, token_ids.T, transform_weight, transform_bias.reshape(1, DM), norm_gain.reshape(1, DM),
        norm_bias.reshape(1, DM), decoder_weight, decoder_bias.reshape(1, VL), cand, occupancy, doc_blocks,
    )
    return weights, picked.transpose(2, 0, 1)


def solution(mesh):
    placed = (
        P("doc", None, None),
        P("doc", None),
        P(),
        P(),
        P(),
        P(),
        P(None, "term"),
        P("term"),
        P("doc", None),
        P("doc", "term"),
        P("doc", "term", None, None),
    )
    return jax.shard_map(
        body,
        mesh=mesh,
        in_specs=placed,
        out_specs=(P("doc", "term"), P("doc", None, "term")),
        check_vma=False,
    )
```

time: 288 us -> 72.1 us (0.25)
  local copies, waits for them, and re-layouts: 95 us -> 9.9 us
  waiting for transfers between devices: 82.8 us -> 0 us
  Pallas kernels: 0 us -> 61.1 us
  matrix products: 44.7 us -> 0 us
  other arithmetic: 29.1 us -> 0 us
  blocking collectives: 14.4 us -> 0 us
  between operations: 14.3 us -> 0.66 us
  starting transfers between devices: 6.05 us -> 0 us
    gather x7 -> x0, local copies, waits for them, and re-layouts: 83.1 us -> none  [the longest x2 59 us: body(): jnp.take(all_weights, flat_index.reshape(-1), axis=0)]
    psum x1 -> x0, waiting for transfers between devices: 75.3 us -> none  [body(): score_total = lax.psum(partial_value, 'term')]
    pallas_call x0 -> x1, Pallas kernels: none -> 61.1 us  [body(): pl.pallas_call(kernel, out_shape=(jax.ShapeDtypeStruct((QD, VL), BF), jax...]
    dot_general x3 -> x0, matrix products: 44.7 us -> none  [the longest x1 17.5 us: body(): jnp.dot(query_states.reshape(query_count * query_length, model_width), tr...]
    all_gather x1 -> x0, blocking collectives: 14.4 us -> none  [body(): lax.all_gather(candidates, 'doc', axis=0, tiled=True)]
    mul x2 -> x0, other arithmetic: 14 us -> none  [the longest x1 14 us: body(): buffer.reshape(doc_count, tile_local, MOST, blocks_local, block_terms)]
    another operation x2 -> x0, other arithmetic: 6.68 us -> none  [tile_ranks(): tile_before = jnp.cumsum(tile_hits, axis=-2) - tile_hits]
    all_to_all x1 -> x0, starting transfers between devices: 5.97 us -> none  [body(): lax.all_to_all(score_share, 'doc', split_axis=0, concat_axis=1, tiled=True)]
  transfers between devices with their start and end apart: 3 -> 0, of which waited for: 3 -> 0; matrix products, arithmetic and copies ran while one was open for 9% -> 0% of each run, Pallas kernels for 0% -> 0%
where the time goes in v1:
time: 72.1 us; the launch traced here: 71.6 us
  Pallas kernels  61.1 us (85%)
  local copies, waits for them, and re-layouts  9.9 us (14%)
    pallas_call x1, Pallas kernels, body(): pl.pallas_call(kernel, out_shape=(jax.ShapeDtypeStruct((QD, VL), BF), jax...  61.1 us
    unnamed x2, local copies, waits for them, and re-layouts  3.22 us

profile of v1, /device:TPU:1, one launch (start us, length us, event | category | flops | bytes accessed | tf_op | source)
XLA Modules:
  0.0 71.6 jit_solution(7751299551703861504)
XLA Ops:
  0.6 1.3 %reshape.21.tb_ref = f32[1,768]{1,0:T(1,128)} reshape(f32[768]{0:T(1024)} %param.14) | data formatting | bytes 6144 | tf_op jit(solution)/shard_map/reshape | solution.py:315
  1.9 1.3 %reshape.22.g_ref = f32[1,768]{1,0:T(1,128)} reshape(f32[768]{0:T(1024)} %param.15) | data formatting | bytes 6144 | tf_op jit(solution)/shard_map/reshape | solution.py:315
  3.2 1.3 %reshape.23.nb_ref = f32[1,768]{1,0:T(1,128)} reshape(f32[768]{0:T(1024)} %param.16) | data formatting | bytes 6144 | tf_op jit(solution)/shard_map/reshape | solution.py:316
  4.5 1.3 %reshape.24.db_ref = f32[1,1920]{1,0:T(1,128)} reshape(f32[1920]{0:T(1024)} %param.18) | data formatting | bytes 15360 | tf_op jit(solution)/shard_map/reshape | solution.py:316
  5.7 0.8 %broadcast_in_dim.7 = s32[32,2,32]{2,1,0:T(2,128)S(1)} reshape(s32[32,64]{1,0:T(8,128)} %bitcast.6) | data formatting | bytes 16384 | tf_op jit(solution)/shard_map/broadcast_in_dim | solution.py:270
  6.6 0.7 %reshape.25.cand_ref = s32[2,32,128]{2,1,0:T(8,128)} reshape(s32[2,32,4,32]{3,2,1,0:T(4,128)S(1)} %broadcast_bitcast_fusion) | data formatting | bytes 65536 | tf_op jit(solution)/shard_map/reshape | solution.py:270
  7.3 61.1 %splade.1 = (bf16[64,1920]{1,0:T(8,128)(2,1)}, f32[32,8,64]{2,1,0:T(8,128)}) custom-call(bf16[64,32,768]{2,1,0:T(8,128)(2,1)} %x_hbm.1, s32[32,64]{1,0:T(8,128)} %bitcast.7, bf16[768,768]{1,0:T(8,128)(2,1)} %tw_hbm.1, f32[1,768]{1,0:T(1,128)} %reshape.21.tb_ref, f32[1,768]{1,0:T(1,128)} %reshape.22.g_ref, f32[1,768]{1,0:T(1,128)} %reshape.23.nb_ref, ...), custom_call_target="tpu_custom_call" | custom-call | tf_op jit(solution)/shard_map/splade/pallas_call | solution.py:274
  68.4 1.7 %copy.16 = bf16[64,1920]{1,0:T(8,128)(2,1)} copy(bf16[64,1920]{1,0:T(8,128)(2,1)} %get-tuple-element.8) | data formatting | bytes 491520
  70.1 1.6 %copy.17 = f32[64,32,8]{0,2,1:T(8,128)} copy(f32[64,32,8]{0,2,1:T(8,128)} %bitcast.5) | data formatting | bytes 131072
  (2 shorter events, 0.0 us)

commit v2 on v1

v2 whole, which is shorter than its diff:
```python
import jax
import jax.numpy as jnp
from jax import lax
from jax.experimental import pallas as pl
from jax.experimental.pallas import tpu as pltpu
from jax.sharding import PartitionSpec as P

MESH = pl.DeviceIdType.MESH
VOCAB = 30522
NDOC = 8
NY = 4
NZ = 4
QD = 64
QLEN = 32
DM = 768
VL = 1920
NB = 15
NTL = 16
CAND = 32
CH = 16
TOK = CH * QLEN
HQ = 32
HL = NDOC * HQ
BLOCKS = ((0, 512), (512, 512), (1024, 512), (1536, 384))
PARTS = ((0, 1024), (1024, 896))
BF = jnp.bfloat16
F32 = jnp.float32


def kernel(
    x_hbm, tok_hbm, tw_hbm, tb_hbm, g_hbm, nb_hbm, dw_hbm, db_hbm, occ_hbm, docs_hbm,
    qw_ref, back,
    xv, twv, dwv, dv, tok_ref, tb_ref, g_ref, nb_ref, db_ref, occ_ref,
    occrow, lens, nrm, qw_v, wall, wt, sbuf, rbuf, s2buf, r2buf, pbuf,
    xsem, wsem, dsem, vsem, osem, ag_s, ag_r, ps_s, ps_r, s1_s, s1_r, s2_s, s2_r, rt_s, rt_r,
):
    doc = lax.axis_index("doc")
    term = lax.axis_index("term")
    z = term // NY
    y = lax.rem(term, NY)

    tw_cp = pltpu.make_async_copy(tw_hbm, twv, wsem.at[0])

    def dw_copy(i):
        cols = pl.ds(*BLOCKS[i])
        return pltpu.make_async_copy(dw_hbm.at[:, cols], dwv.at[:, cols], wsem.at[1 + i])

    def x_copy(c):
        return pltpu.make_async_copy(x_hbm.at[pl.ds(c * CH, CH)], xv.at[pl.ds(c * CH, CH)], xsem.at[c])

    def d_copy(b):
        return pltpu.make_async_copy(docs_hbm.at[:, b], dv.at[:, :, pl.ds(b * 128, 128)], dsem.at[b])

    small = [
        pltpu.make_async_copy(a, b, vsem.at[n])
        for n, (a, b) in enumerate((
            (tok_hbm, tok_ref), (tb_hbm, tb_ref), (g_hbm, g_ref), (nb_hbm, nb_ref), (db_hbm, db_ref), (occ_hbm, occ_ref),
        ))
    ]
    tw_cp.start()
    x_copy(0).start()
    for cp in small:
        cp.start()
    for i in range(len(BLOCKS)):
        dw_copy(i).start()
    for c in range(1, 4):
        x_copy(c).start()
    for b in range(NB):
        d_copy(b).start()

    barrier = pltpu.get_barrier_semaphore()
    for k in range(1, NDOC):
        pl.semaphore_signal(barrier, inc=1, device_id={"doc": lax.rem(doc + k, NDOC)}, device_id_type=MESH)
    for k in range(1, 4):
        pl.semaphore_signal(barrier, inc=1, device_id={"term": z * NY + lax.rem(y + k, NY)}, device_id_type=MESH)
        pl.semaphore_signal(barrier, inc=1, device_id={"term": lax.rem(z + k, NZ) * NY + y}, device_id_type=MESH)

    for cp in small:
        cp.wait()

    live = jnp.where(tok_ref[...] != 0, 1.0, 0.0).astype(BF)
    lens[...] = lax.dot_general(
        live, jnp.ones((QLEN, 128), BF), (((0,), (0,)), ((), ())), preferred_element_type=F32
    )
    spread = jnp.where(
        lax.broadcasted_iota(jnp.int32, (NB, VL), 1) // 128 == lax.broadcasted_iota(jnp.int32, (NB, VL), 0), 1.0, 0.0
    ).astype(BF)
    occrow[...] = jnp.dot(occ_ref[...].astype(F32).astype(BF), spread, preferred_element_type=F32)

    def row(ref):
        return jnp.concatenate([ref[i:i + 1, :] for i in range(ref.shape[0])], axis=1)

    tb, gain, nbias, dbias = row(tb_ref), row(g_ref), row(nb_ref), row(db_ref)
    sibling = doc + 1 - 2 * lax.rem(doc, 2)

    def ag_copy(c, k, part):
        half, sub = c // 2, lax.rem(c, 2)
        place = wall.at[half, doc, pl.ds(sub * CH, CH), pl.ds(*PARTS[part])]
        return pltpu.make_async_remote_copy(
            src_ref=place, dst_ref=place, send_sem=ag_s.at[c, k, part], recv_sem=ag_r.at[c, k, part],
            device_id={"doc": sibling if k == 0 else lax.rem(doc + 2 * k, NDOC)}, device_id_type=MESH,
        )

    def pass_copy(c, k):
        half, sub = c // 2, lax.rem(c, 2)
        place = wall.at[half, lax.rem(doc + NDOC - 2 * k, NDOC), pl.ds(sub * CH, CH)]
        return pltpu.make_async_remote_copy(
            src_ref=place, dst_ref=place, send_sem=ps_s.at[c, k - 1], recv_sem=ps_r.at[c, k - 1],
            device_id={"doc": sibling}, device_id_type=MESH,
        )

    def expand(c):
        x_copy(c).wait()
        rows = pl.ds(pl.multiple_of(c * CH, CH), CH)
        h = jnp.dot(xv[rows].reshape(TOK, DM), twv[...], preferred_element_type=F32) + tb
        h = 0.5 * h * (1.0 + lax.erf(h * 0.7071067811865476))
        cen = h - jnp.mean(h, axis=-1, keepdims=True)
        var = jnp.mean(cen * cen, axis=-1, keepdims=True)
        n = cen * lax.rsqrt(var + 1e-6) * gain + nbias
        n3 = n.reshape(CH, QLEN, DM)
        pos = lax.broadcasted_iota(jnp.int32, (CH, QLEN, DM), 1).astype(F32)
        length = jnp.concatenate([lens[rows, :]] * (DM // 128), axis=1)
        n3 = jnp.where(pos < length[:, None, :], n3, n3[:, 0:1, :])
        nrm[...] = n3.reshape(TOK, DM).astype(BF)

    def decode(c):
        half, sub = c // 2, lax.rem(c, 2)
        rows = pl.ds(pl.multiple_of(c * CH, CH), CH)
        srow = pl.ds(pl.multiple_of(sub * CH, CH), CH)
        for c0, COLS in BLOCKS:
            lg = jnp.dot(nrm[...], dwv[:, c0:c0 + COLS], preferred_element_type=F32)
            top = jnp.max(lg.reshape(CH, QLEN, COLS), axis=1) + dbias[:, c0:c0 + COLS]
            w = jnp.log1p(jnp.maximum(top, 0.0))
            col = term * VL + c0 + lax.broadcasted_iota(jnp.int32, (CH, COLS), 1)
            w = jnp.where(col < VOCAB, w, 0.0).astype(BF)
            wall[half, doc, srow, c0:c0 + COLS] = w
            qw_v[rows, c0:c0 + COLS] = w
            for part, (p0, width) in enumerate(PARTS):
                if c0 + COLS == p0 + width:
                    for k in (2, 1, 3, 0):
                        ag_copy(c, k, part).start()

    def ag_pass(c):
        for k in (1, 3, 2):
            for part in range(2):
                ag_copy(c, k, part).wait_recv()
            pass_copy(c, k).start()

    def ag_wait(c):
        for part in range(2):
            ag_copy(c, 0, part).wait_recv()
        for k in (1, 3, 2):
            pass_copy(c, k).wait_recv()

    def ag_sent(c):
        for k in range(4):
            for part in range(2):
                ag_copy(c, k, part).wait_send()
        for k in (1, 3, 2):
            pass_copy(c, k).wait_send()

    def peers(k):
        py = lax.rem(y + k + 1, NY)
        pz = lax.rem(z + k + 1, NZ)
        return (py, {"term": z * NY + py}), (pz, {"term": pz * NY + y})

    def s1_copy(half, axis, i, k):
        peer, to = peers(k)[axis]
        return pltpu.make_async_remote_copy(
            src_ref=sbuf.at[half, axis, i, peer], dst_ref=rbuf.at[half, axis, i, k],
            send_sem=s1_s.at[half, axis, i, k], recv_sem=s1_r.at[half, axis, i, k], device_id=to, device_id_type=MESH,
        )

    def s2_copy(half, axis, i, k):
        peer, to = peers(k)[1 - axis]
        return pltpu.make_async_remote_copy(
            src_ref=s2buf.at[half, axis, i, peer], dst_ref=r2buf.at[half, axis, i, k],
            send_sem=s2_s.at[half, axis, i, k], recv_sem=s2_r.at[half, axis, i, k], device_id=to, device_id_type=MESH,
        )


    def rt_copy(half, k):
        peer = lax.rem(doc + k + 1, NDOC)
        return pltpu.make_async_remote_copy(
            src_ref=pbuf.at[half, peer], dst_ref=back.at[half, doc],
            send_sem=rt_s.at[half, k], recv_sem=rt_r.at[half, k], device_id={"doc": peer}, device_id_type=MESH,
        )

    def own_copy(half):
        return pltpu.make_async_copy(pbuf.at[half, doc], back.at[half, doc], osem.at[half])

    def give_back(half):
        for k in range(NDOC - 1):
            rt_copy(half, k).start()
        own_copy(half).start()

    def score(half, masked, between):
        for c0 in range(0, VL, 128):
            part = wall[half, :, :, c0:c0 + 128].reshape(HL, 128)
            wt[c0:c0 + 128, :] = part.T

        @pl.loop(0, 2)
        def _(i):
            for axis in range(2):
                first = pl.multiple_of((2 * i + axis) * 4, 4)
                if masked:
                    for t in range(4):
                        keep = occrow[pl.ds(first + t, 1), :].astype(BF)
                        dv[first + t] = dv[first + t] * keep
                docs = dv[pl.ds(first, 4)].reshape(512, VL)
                r = jnp.dot(docs, wt[...], preferred_element_type=F32).reshape(4, NZ, NY, 8, HL)
                for zz in range(NZ):
                    for yy in range(NY):
                        part = jnp.concatenate([r[t, zz, yy] for t in range(4)], axis=0).astype(BF)
                        slot, at = (yy, zz) if axis == 0 else (zz, yy)
                        sbuf[half, axis, i, slot, at] = part
                for k in (1, 0, 2):
                    s1_copy(half, axis, i, k).start()
            if between is not None:
                @pl.when(i == 0)
                def _():
                    between()

    def reduce1(half, i, axis):
        for k in (0, 2, 1):
            s1_copy(half, axis, i, k).wait_recv()
        tot = sbuf[half, axis, i, y if axis == 0 else z].astype(F32)
        for k in range(3):
            tot = tot + rbuf[half, axis, i, k].astype(F32)
        s2buf[half, axis, i] = tot.astype(BF)
        for k in (1, 0, 2):
            s2_copy(half, axis, i, k).start()

    def reduce2(half, i, axis):
        lane_group = lax.broadcasted_iota(jnp.int32, (8, 128), 1) // HQ
        for k in (0, 2, 1):
            s2_copy(half, axis, i, k).wait_recv()
        tot = s2buf[half, axis, i, z if axis == 0 else y].astype(F32)
        for k in range(3):
            tot = tot + r2buf[half, axis, i, k].astype(F32)
        for j in range(NDOC):
            made = jnp.zeros((8, 128), F32)
            for t in range(4):
                piece = tot[t * 8:(t + 1) * 8, (j // 4) * 128:(j // 4 + 1) * 128]
                turn = ((t - j % 4) * HQ) % 128
                if turn:
                    piece = pltpu.roll(piece, turn, 1)
                made = jnp.where(lane_group == t, piece, made)
            pbuf[half, j, 2 * i + axis] = made

    tw_cp.wait()

    @pl.loop(0, 4)
    def _(c):
        expand(c)

        @pl.when(c == 0)
        def _():
            for i in range(len(BLOCKS)):
                dw_copy(i).wait()
            pl.semaphore_wait(barrier, NDOC - 1 + 6)

        @pl.when(c >= 2)
        def _():
            ag_pass(c - 2)

        decode(c)

    qw_cp = pltpu.make_async_copy(qw_v, qw_ref, osem.at[2])
    qw_cp.start()
    for b in range(NB):
        d_copy(b).wait()
    ag_wait(0)
    ag_wait(1)
    score(0, True, lambda: ag_pass(2))
    ag_pass(3)
    for c in range(3):
        ag_sent(c)
    ag_wait(2)
    ag_wait(3)
    score(1, False, None)
    ag_sent(3)
    groups = [(half, i, axis) for half in range(2) for i in range(2) for axis in range(2)]
    for group in groups:
        reduce1(*group)
    for half, i, axis in groups:
        for k in range(3):
            s1_copy(half, axis, i, k).wait_send()
    for n, group in enumerate(groups):
        reduce2(*group)
        if n in (3, 7):
            give_back(n // 4)
    for half, i, axis in groups:
        for k in range(3):
            s2_copy(half, axis, i, k).wait_send()
    qw_cp.wait()
    for half in range(2):
        own_copy(half).wait()
        for k in range(NDOC - 1):
            rt_copy(half, k).wait()


def pick(qw_ref, back, cand_ref, qw_out, out_ref, want):
    qw_out[...] = qw_ref[...]
    part = lax.broadcasted_iota(jnp.int32, (CAND, 128), 1) // HQ
    for half in range(2):
        mine = cand_ref[:, half * HQ:(half + 1) * HQ]
        want[half] = jnp.concatenate([mine] * 4, axis=1) - part

    @pl.loop(0, CAND // 8)
    def _(block):
        made = []
        for half in range(2):
            rows = want[half, pl.ds(pl.multiple_of(block * 8, 8), 8), :]
            each = [jnp.broadcast_to(rows[i:i + 1, :], (8, 128)) for i in range(8)]
            accs = [jnp.zeros((8, 128), F32) for _ in range(8)]
            for e in range(NDOC * 4):
                found = back[half, e // 4, e % 4]
                for i in range(8):
                    accs[i] = jnp.where(each[i] == 4 * e, found, accs[i])
            for i in range(8):
                acc = accs[i] + pltpu.roll(accs[i], 64, 1)
                made.append(acc + pltpu.roll(acc, 32, 1))
        for i in range(8):
            out_ref[block * 8 + i, :, 0:HQ] = made[i][:, 0:HQ]
            out_ref[block * 8 + i, :, HQ:2 * HQ] = made[8 + i][:, HQ:2 * HQ]


def body(
    query_states, token_ids, transform_weight, transform_bias, norm_gain, norm_bias,
    decoder_weight, decoder_bias, candidates, occupancy, doc_blocks,
):
    any_ = pl.BlockSpec(memory_space=pl.ANY)
    vm = pl.BlockSpec(memory_space=pltpu.VMEM)
    dma = pltpu.SemaphoreType.DMA
    weights, back = pl.pallas_call(
        kernel,
        out_shape=(
            jax.ShapeDtypeStruct((QD, VL), BF),
            jax.ShapeDtypeStruct((2, NDOC, 4, 8, 128), F32),
        ),
        in_specs=[any_] * 10,
        out_specs=(any_, any_),
        scratch_shapes=[
            pltpu.VMEM((QD, QLEN, DM), BF),
            pltpu.VMEM((DM, DM), BF),
            pltpu.VMEM((DM, VL), BF),
            pltpu.VMEM((NTL, 128, VL), BF),
            pltpu.VMEM((QLEN, QD), jnp.int32),
            pltpu.VMEM((6, 128), F32),
            pltpu.VMEM((6, 128), F32),
            pltpu.VMEM((6, 128), F32),
            pltpu.VMEM((NB, 128), F32),
            pltpu.VMEM((NTL, NB), jnp.int32),
            pltpu.VMEM((NTL, VL), F32),
            pltpu.VMEM((QD, 128), F32),
            pltpu.VMEM((TOK, DM), BF),
            pltpu.VMEM((QD, VL), BF),
            pltpu.VMEM((2, NDOC, HQ, VL), BF),
            pltpu.VMEM((VL, HL), BF),
            pltpu.VMEM((2, 2, 2, 4, 4, 32, HL), BF),
            pltpu.VMEM((2, 2, 2, 3, 4, 32, HL), BF),
            pltpu.VMEM((2, 2, 2, 4, 32, HL), BF),
            pltpu.VMEM((2, 2, 2, 3, 32, HL), BF),
            pltpu.VMEM((2, NDOC, 4, 8, 128), F32),
            dma((4,)),
            dma((1 + len(BLOCKS),)),
            dma((NB,)),
            dma((6,)),
            dma((3,)),
            dma((4, 4, 2)),
            dma((4, 4, 2)),
            dma((4, 3)),
            dma((4, 3)),
            dma((2, 2, 2, 3)),
            dma((2, 2, 2, 3)),
            dma((2, 2, 2, 3)),
            dma((2, 2, 2, 3)),
            dma((2, NDOC - 1)),
            dma((2, NDOC - 1)),
        ],
        compiler_params=pltpu.CompilerParams(
            collective_id=0, has_side_effects=True, vmem_limit_bytes=60 * 1024 * 1024
        ),
        name="splade",
    )(
        query_states, token_ids.T, transform_weight, transform_bias.reshape(6, 128), norm_gain.reshape(6, 128),
        norm_bias.reshape(6, 128), decoder_weight, decoder_bias.reshape(NB, 128), occupancy, doc_blocks,
    )
    weights, picked = pl.pallas_call(
        pick,
        out_shape=(
            jax.ShapeDtypeStruct((QD, VL), BF),
            jax.ShapeDtypeStruct((CAND, 8, QD), F32),
        ),
        in_specs=[vm, vm, vm],
        out_specs=(vm, vm),
        scratch_shapes=[pltpu.VMEM((2, CAND, 128), jnp.int32)],
        name="pick",
    )(weights, back, candidates.T)
    return weights, picked.transpose(2, 0, 1)


def solution(mesh):
    placed = (
        P("doc", None, None),
        P("doc", None),
        P(),
        P(),
        P(),
        P(),
        P(None, "term"),
        P("term"),
        P("doc", None),
        P("doc", "term"),
        P("doc", "term", None, None),
    )
    return jax.shard_map(
        body,
        mesh=mesh,
        in_specs=placed,
        out_specs=(P("doc", "term"), P("doc", None, "term")),
        check_vma=False,
    )
```

time: 72.1 us -> 54 us (0.75)
  local copies, waits for them, and re-layouts: 9.9 us -> 0 us
  Pallas kernels: 61.1 us -> 53.2 us
    pallas_call x1, Pallas kernels: 61.1 us -> 50.3 us  [body(): pl.pallas_call(kernel, out_shape=(jax.ShapeDtypeStruct((QD, VL), BF), jax...]
    reshape x5 -> x0, local copies, waits for them, and re-layouts: 5.85 us -> none  [the longest x1 1.3 us: body(): decoder_bias.reshape(1, VL)]
    unnamed x2 -> x0, local copies, waits for them, and re-layouts: 3.22 us -> none
    pallas_call x0 -> x1, Pallas kernels: none -> 2.92 us  [body(): pl.pallas_call(pick, out_shape=(jax.ShapeDtypeStruct((QD, VL), BF), jax.S...]
    broadcast_in_dim x2 -> x0, local copies, waits for them, and re-layouts: 0.81 us -> none  [body(): jnp.broadcast_to(cand, (CAND, 2, 4, HQ)).transpose(1, 0, 2, 3)]
where the time goes in v2:
time: 54 us; the launch traced here: 53.9 us
  Pallas kernels  53.2 us (99%)
  between operations  0.64 us (1%)
    pallas_call x1, Pallas kernels, body(): pl.pallas_call(kernel, out_shape=(jax.ShapeDtypeStruct((QD, VL), BF), jax...  50.3 us
    pallas_call x1, Pallas kernels, body(): pl.pallas_call(pick, out_shape=(jax.ShapeDtypeStruct((QD, VL), BF), jax.S...  2.92 us

profile of v2, /device:TPU:1, one launch (start us, length us, event | category | flops | bytes accessed | tf_op | source)
XLA Modules:
  0.0 53.9 jit_solution(7589110301452552626)
XLA Ops:
  0.6 50.3 %splade.1 = (bf16[64,1920]{1,0:T(8,128)(2,1)}, f32[2,8,4,8,128]{4,3,2,1,0:T(8,128)}) custom-call(bf16[64,32,768]{2,1,0:T(8,128)(2,1)} %x_hbm.1, s32[32,64]{1,0:T(8,128)} %bitcast.8, bf16[768,768]{1,0:T(8,128)(2,1)} %tw_hbm.1, f32[6,128]{1,0:T(8,128)} %bitcast.10, f32[6,128]{1,0:T(8,128)} %bitcast.11, f32[6,128]{1,0:T(8,128)} %bitcast.12, ...), custom_call_target="tpu_custom_call" | custom-call | tf_op jit(solution)/shard_map/splade/pallas_call | solution.py:336
  50.9 2.9 %pick.1 = (bf16[64,1920]{1,0:T(8,128)(2,1)}, f32[32,8,64]{2,1,0:T(8,128)}) custom-call(bf16[64,1920]{1,0:T(8,128)(2,1)} %get-tuple-element.6.qw_ref, f32[2,8,4,8,128]{4,3,2,1,0:T(8,128)} %get-tuple-element.7.back, s32[32,64]{1,0:T(8,128)} %bitcast.7), custom_call_target="tpu_custom_call" | custom-call | tf_op jit(solution)/shard_map/pick/pallas_call | solution.py:390

commit v3 on v2

--- a/solution.py
+++ b/solution.py
@@ -32,7 +32,7 @@
     qw_ref, back,
     xv, twv, dwv, dv, tok_ref, tb_ref, g_ref, nb_ref, db_ref, occ_ref,
     occrow, lens, nrm, qw_v, wall, wt, sbuf, rbuf, s2buf, r2buf, pbuf,
-    xsem, wsem, dsem, vsem, osem, ag_s, ag_r, ps_s, ps_r, s1_s, s1_r, s2_s, s2_r, rt_s, rt_r,
+    xsem, wsem, dsem, vsem, osem, ag_s, ag_r, s1_s, s1_r, s2_s, s2_r, rt_s, rt_r,
 ):
     doc = lax.axis_index("doc")
     term = lax.axis_index("term")
@@ -42,14 +42,14 @@
     tw_cp = pltpu.make_async_copy(tw_hbm, twv, wsem.at[0])
 
     def dw_copy(i):
-        cols = pl.ds(*BLOCKS[i])
-        return pltpu.make_async_copy(dw_hbm.at[:, cols], dwv.at[:, cols], wsem.at[1 + i])
+        part = pl.ds(i * (DM // 4), DM // 4)
+        return pltpu.make_async_copy(dw_hbm.at[part], dwv.at[part], wsem.at[1])
 
     def x_copy(c):
         return pltpu.make_async_copy(x_hbm.at[pl.ds(c * CH, CH)], xv.at[pl.ds(c * CH, CH)], xsem.at[c])
 
     def d_copy(b):
-        return pltpu.make_async_copy(docs_hbm.at[:, b], dv.at[:, :, pl.ds(b * 128, 128)], dsem.at[b])
+        return pltpu.make_async_copy(docs_hbm.at[:, b], dv.at[:, :, pl.ds(b * 128, 128)], dsem)
 
     small = [
         pltpu.make_async_copy(a, b, vsem.at[n])
@@ -61,13 +61,10 @@
     x_copy(0).start()
     for cp in small:
         cp.start()
-    for i in range(len(BLOCKS)):
+    for i in range(4):
         dw_copy(i).start()
     for c in range(1, 4):
         x_copy(c).start()
-    for b in range(NB):
-        d_copy(b).start()
-
     barrier = pltpu.get_barrier_semaphore()
     for k in range(1, NDOC):
         pl.semaphore_signal(barrier, inc=1, device_id={"doc": lax.rem(doc + k, NDOC)}, device_id_type=MESH)
@@ -82,10 +79,12 @@
     lens[...] = lax.dot_general(
         live, jnp.ones((QLEN, 128), BF), (((0,), (0,)), ((), ())), preferred_element_type=F32
     )
-    spread = jnp.where(
-        lax.broadcasted_iota(jnp.int32, (NB, VL), 1) // 128 == lax.broadcasted_iota(jnp.int32, (NB, VL), 0), 1.0, 0.0
-    ).astype(BF)
-    occrow[...] = jnp.dot(occ_ref[...].astype(F32).astype(BF), spread, preferred_element_type=F32)
+
+    def occupancy_rows():
+        spread = jnp.where(
+            lax.broadcasted_iota(jnp.int32, (NB, VL), 1) // 128 == lax.broadcasted_iota(jnp.int32, (NB, VL), 0), 1.0, 0.0
+        ).astype(BF)
+        occrow[...] = jnp.dot(occ_ref[...].astype(F32).astype(BF), spread, preferred_element_type=F32)
 
     def row(ref):
         return jnp.concatenate([ref[i:i + 1, :] for i in range(ref.shape[0])], axis=1)
@@ -97,7 +96,7 @@
         half, sub = c // 2, lax.rem(c, 2)
         place = wall.at[half, doc, pl.ds(sub * CH, CH), pl.ds(*PARTS[part])]
         return pltpu.make_async_remote_copy(
-            src_ref=place, dst_ref=place, send_sem=ag_s.at[c, k, part], recv_sem=ag_r.at[c, k, part],
+            src_ref=place, dst_ref=place, send_sem=ag_s.at[c], recv_sem=ag_r.at[c, 0 if k else 1],
             device_id={"doc": sibling if k == 0 else lax.rem(doc + 2 * k, NDOC)}, device_id_type=MESH,
         )
 
@@ -105,7 +104,7 @@
         half, sub = c // 2, lax.rem(c, 2)
         place = wall.at[half, lax.rem(doc + NDOC - 2 * k, NDOC), pl.ds(sub * CH, CH)]
         return pltpu.make_async_remote_copy(
-            src_ref=place, dst_ref=place, send_sem=ps_s.at[c, k - 1], recv_sem=ps_r.at[c, k - 1],
+            src_ref=place, dst_ref=place, send_sem=ag_s.at[c], recv_sem=ag_r.at[c, 1],
             device_id={"doc": sibling}, device_id_type=MESH,
         )
 
@@ -140,50 +139,70 @@
                     for k in (2, 1, 3, 0):
                         ag_copy(c, k, part).start()
 
+    def ag_rows(c, count, kind):
+        rows = wall.at[c // 2, pl.ds(0, count), pl.ds(lax.rem(c, 2) * CH, CH)]
+        return pltpu.make_async_remote_copy(
+            src_ref=rows, dst_ref=rows, send_sem=ag_s.at[c], recv_sem=ag_r.at[c, kind],
+            device_id={"doc": sibling}, device_id_type=MESH,
+        )
+
     def ag_pass(c):
+        ag_rows(c, 3, 0).wait_recv()
         for k in (1, 3, 2):
-            for part in range(2):
-                ag_copy(c, k, part).wait_recv()
             pass_copy(c, k).start()
 
     def ag_wait(c):
-        for part in range(2):
-            ag_copy(c, 0, part).wait_recv()
-        for k in (1, 3, 2):
-            pass_copy(c, k).wait_recv()
+        ag_rows(c, 4, 1).wait_recv()
 
     def ag_sent(c):
-        for k in range(4):
-            for part in range(2):
-                ag_copy(c, k, part).wait_send()
-        for k in (1, 3, 2):
-            pass_copy(c, k).wait_send()
-
-    def peers(k):
+        ag_rows(c, 7, 0).wait_send()
+
+    def peer_on(first, k):
         py = lax.rem(y + k + 1, NY)
         pz = lax.rem(z + k + 1, NZ)
-        return (py, {"term": z * NY + py}), (pz, {"term": pz * NY + y})
+        return first * py + (1 - first) * pz, first * (z * NY + py) + (1 - first) * (pz * NY + y)
 
     def s1_copy(half, axis, i, k):
-        peer, to = peers(k)[axis]
+        peer, to = peer_on(1 - axis, k)
         return pltpu.make_async_remote_copy(
             src_ref=sbuf.at[half, axis, i, peer], dst_ref=rbuf.at[half, axis, i, k],
-            send_sem=s1_s.at[half, axis, i, k], recv_sem=s1_r.at[half, axis, i, k], device_id=to, device_id_type=MESH,
+            send_sem=s1_s.at[half, axis, i], recv_sem=s1_r.at[half, axis, i],
+            device_id={"term": to}, device_id_type=MESH,
         )
 
     def s2_copy(half, axis, i, k):
-        peer, to = peers(k)[1 - axis]
+        peer, to = peer_on(axis, k)
         return pltpu.make_async_remote_copy(
             src_ref=s2buf.at[half, axis, i, peer], dst_ref=r2buf.at[half, axis, i, k],
-            send_sem=s2_s.at[half, axis, i, k], recv_sem=s2_r.at[half, axis, i, k], device_id=to, device_id_type=MESH,
-        )
-
+            send_sem=s2_s.at[half, axis, i], recv_sem=s2_r.at[half, axis, i],
+            device_id={"term": to}, device_id_type=MESH,
+        )
+
+    def s1_all(half, axis, i):
+        return pltpu.make_async_remote_copy(
+            src_ref=sbuf.at[half, axis, i, pl.ds(0, 3)], dst_ref=rbuf.at[half, axis, i],
+            send_sem=s1_s.at[half, axis, i], recv_sem=s1_r.at[half, axis, i],
+            device_id={"doc": sibling}, device_id_type=MESH,
+        )
+
+    def s2_all(half, axis, i):
+        return pltpu.make_async_remote_copy(
+            src_ref=s2buf.at[half, axis, i, pl.ds(0, 3)], dst_ref=r2buf.at[half, axis, i],
+            send_sem=s2_s.at[half, axis, i], recv_sem=s2_r.at[half, axis, i],
+            device_id={"doc": sibling}, device_id_type=MESH,
+        )
+
+    def rt_all(half):
+        return pltpu.make_async_remote_copy(
+            src_ref=pbuf.at[half, pl.ds(0, NDOC - 1)], dst_ref=back.at[half, pl.ds(0, NDOC - 1)],
+            send_sem=rt_s.at[half], recv_sem=rt_r.at[half], device_id={"doc": sibling}, device_id_type=MESH,
+        )
 
     def rt_copy(half, k):
         peer = lax.rem(doc + k + 1, NDOC)
         return pltpu.make_async_remote_copy(
             src_ref=pbuf.at[half, peer], dst_ref=back.at[half, doc],
-            send_sem=rt_s.at[half, k], recv_sem=rt_r.at[half, k], device_id={"doc": peer}, device_id_type=MESH,
+            send_sem=rt_s.at[half], recv_sem=rt_r.at[half], device_id={"doc": peer}, device_id_type=MESH,
         )
 
     def own_copy(half):
@@ -194,48 +213,43 @@
             rt_copy(half, k).start()
         own_copy(half).start()
 
-    def score(half, masked, between):
+    def weights_of(half):
         for c0 in range(0, VL, 128):
             part = wall[half, :, :, c0:c0 + 128].reshape(HL, 128)
             wt[c0:c0 + 128, :] = part.T
 
-        @pl.loop(0, 2)
-        def _(i):
-            for axis in range(2):
-                first = pl.multiple_of((2 * i + axis) * 4, 4)
-                if masked:
-                    for t in range(4):
-                        keep = occrow[pl.ds(first + t, 1), :].astype(BF)
-                        dv[first + t] = dv[first + t] * keep
-                docs = dv[pl.ds(first, 4)].reshape(512, VL)
-                r = jnp.dot(docs, wt[...], preferred_element_type=F32).reshape(4, NZ, NY, 8, HL)
-                for zz in range(NZ):
-                    for yy in range(NY):
-                        part = jnp.concatenate([r[t, zz, yy] for t in range(4)], axis=0).astype(BF)
-                        slot, at = (yy, zz) if axis == 0 else (zz, yy)
-                        sbuf[half, axis, i, slot, at] = part
-                for k in (1, 0, 2):
-                    s1_copy(half, axis, i, k).start()
-            if between is not None:
-                @pl.when(i == 0)
-                def _():
-                    between()
+    def score(half, i, axis):
+        first = pl.multiple_of((2 * i + axis) * 4, 4)
+
+        @pl.when(half == 0)
+        def _():
+            for t in range(4):
+                keep = occrow[pl.ds(first + t, 1), :].astype(BF)
+                dv[first + t] = dv[first + t] * keep
+
+        docs = dv[pl.ds(first, 4)].reshape(512, VL)
+        r = jnp.dot(docs, wt[...], preferred_element_type=F32).reshape(4, NZ, NY, 8, HL)
+        for zz in range(NZ):
+            for yy in range(NY):
+                part = jnp.concatenate([r[t, zz, yy] for t in range(4)], axis=0).astype(BF)
+                sbuf[half, axis, i, yy + axis * (zz - yy), zz + axis * (yy - zz)] = part
+        for k in (1, 0, 2):
+            s1_copy(half, axis, i, k).start()
 
     def reduce1(half, i, axis):
-        for k in (0, 2, 1):
-            s1_copy(half, axis, i, k).wait_recv()
-        tot = sbuf[half, axis, i, y if axis == 0 else z].astype(F32)
+        s1_all(half, axis, i).wait_recv()
+        tot = sbuf[half, axis, i, y + axis * (z - y)].astype(F32)
         for k in range(3):
             tot = tot + rbuf[half, axis, i, k].astype(F32)
         s2buf[half, axis, i] = tot.astype(BF)
         for k in (1, 0, 2):
             s2_copy(half, axis, i, k).start()
+        s1_all(half, axis, i).wait_send()
 
     def reduce2(half, i, axis):
         lane_group = lax.broadcasted_iota(jnp.int32, (8, 128), 1) // HQ
-        for k in (0, 2, 1):
-            s2_copy(half, axis, i, k).wait_recv()
-        tot = s2buf[half, axis, i, z if axis == 0 else y].astype(F32)
+        s2_all(half, axis, i).wait_recv()
+        tot = s2buf[half, axis, i, z + axis * (y - z)].astype(F32)
         for k in range(3):
             tot = tot + r2buf[half, axis, i, k].astype(F32)
         for j in range(NDOC):
@@ -256,9 +270,10 @@
 
         @pl.when(c == 0)
         def _():
-            for i in range(len(BLOCKS)):
-                dw_copy(i).wait()
+            pltpu.make_async_copy(dwv, dwv, wsem.at[1]).wait()
             pl.semaphore_wait(barrier, NDOC - 1 + 6)
+            for b in range(NB):
+                d_copy(b).start()
 
         @pl.when(c >= 2)
         def _():
@@ -268,36 +283,51 @@
 
     qw_cp = pltpu.make_async_copy(qw_v, qw_ref, osem.at[2])
     qw_cp.start()
-    for b in range(NB):
-        d_copy(b).wait()
-    ag_wait(0)
-    ag_wait(1)
-    score(0, True, lambda: ag_pass(2))
-    ag_pass(3)
-    for c in range(3):
+    occupancy_rows()
+    pltpu.make_async_copy(dv, dv, dsem).wait()
+
+    @pl.loop(0, 2)
+    def _(half):
+        @pl.when(half == 1)
+        def _():
+            ag_pass(3)
+
+        ag_wait(2 * half)
+        ag_wait(2 * half + 1)
+        weights_of(half)
+
+        @pl.loop(0, 4)
+        def _(n):
+            score(half, n // 2, lax.rem(n, 2))
+
+            @pl.when((half == 0) & (n == 1))
+            def _():
+                ag_pass(2)
+
+    @pl.loop(0, 8)
+    def _(n):
+        reduce1(n // 4, lax.rem(n // 2, 2), lax.rem(n, 2))
+
+    @pl.loop(0, 4)
+    def _(c):
         ag_sent(c)
-    ag_wait(2)
-    ag_wait(3)
-    score(1, False, None)
-    ag_sent(3)
-    groups = [(half, i, axis) for half in range(2) for i in range(2) for axis in range(2)]
-    for group in groups:
-        reduce1(*group)
-    for half, i, axis in groups:
-        for k in range(3):
-            s1_copy(half, axis, i, k).wait_send()
-    for n, group in enumerate(groups):
-        reduce2(*group)
-        if n in (3, 7):
-            give_back(n // 4)
-    for half, i, axis in groups:
-        for k in range(3):
-            s2_copy(half, axis, i, k).wait_send()
+
+    @pl.loop(0, 2)
+    def _(half):
+        @pl.loop(0, 4)
+        def _(n):
+            reduce2(half, n // 2, lax.rem(n, 2))
+
+        give_back(half)
+
+    @pl.loop(0, 8)
+    def _(n):
+        s2_all(n // 4, lax.rem(n, 2), lax.rem(n // 2, 2)).wait_send()
+
     qw_cp.wait()
     for half in range(2):
         own_copy(half).wait()
-        for k in range(NDOC - 1):
-            rt_copy(half, k).wait()
+        rt_all(half).wait()
 
 
 def pick(qw_ref, back, cand_ref, qw_out, out_ref, want):
@@ -364,20 +394,18 @@
             pltpu.VMEM((2, 2, 2, 3, 32, HL), BF),
             pltpu.VMEM((2, NDOC, 4, 8, 128), F32),
             dma((4,)),
-            dma((1 + len(BLOCKS),)),
-            dma((NB,)),
+            dma((2,)),
+            dma(()),
             dma((6,)),
             dma((3,)),
-            dma((4, 4, 2)),
-            dma((4, 4, 2)),
-            dma((4, 3)),
-            dma((4, 3)),
-            dma((2, 2, 2, 3)),
-            dma((2, 2, 2, 3)),
-            dma((2, 2, 2, 3)),
-            dma((2, 2, 2, 3)),
-            dma((2, NDOC - 1)),
-            dma((2, NDOC - 1)),
+            dma((4,)),
+            dma((4, 2)),
+            dma((2, 2, 2)),
+            dma((2, 2, 2)),
+            dma((2, 2, 2)),
+            dma((2, 2, 2)),
+            dma((2,)),
+            dma((2,)),
         ],
         compiler_params=pltpu.CompilerParams(
             collective_id=0, has_side_effects=True, vmem_limit_bytes=60 * 1024 * 1024

time: 54 us -> 50.9 us (0.943)
  Pallas kernels: 53.2 us -> 50.1 us
    pallas_call x1, Pallas kernels: 50.3 us -> 47.1 us  [body(): pl.pallas_call(kernel, out_shape=(jax.ShapeDtypeStruct((QD, VL), BF), jax...]
where the time goes in v3:
time: 50.9 us; the launch traced here: 50.7 us
  Pallas kernels  50.1 us (98%)
  between operations  0.64 us (1%)
    pallas_call x1, Pallas kernels, body(): pl.pallas_call(kernel, out_shape=(jax.ShapeDtypeStruct((QD, VL), BF), jax...  47.1 us
    pallas_call x1, Pallas kernels, body(): pl.pallas_call(pick, out_shape=(jax.ShapeDtypeStruct((QD, VL), BF), jax.S...  2.92 us

profile of v3, /device:TPU:1, one launch (start us, length us, event | category | flops | bytes accessed | tf_op | source)
XLA Modules:
  0.0 50.7 jit_solution(5217399268631093267)
XLA Ops:
  0.6 47.1 %splade.1 = (bf16[64,1920]{1,0:T(8,128)(2,1)}, f32[2,8,4,8,128]{4,3,2,1,0:T(8,128)}) custom-call(bf16[64,32,768]{2,1,0:T(8,128)(2,1)} %x_hbm.1, s32[32,64]{1,0:T(8,128)} %bitcast.8, bf16[768,768]{1,0:T(8,128)(2,1)} %tw_hbm.1, f32[6,128]{1,0:T(8,128)} %bitcast.10, f32[6,128]{1,0:T(8,128)} %bitcast.11, f32[6,128]{1,0:T(8,128)} %bitcast.12, ...), custom_call_target="tpu_custom_call" | custom-call | tf_op jit(solution)/shard_map/splade/pallas_call | solution.py:366
  47.8 2.9 %pick.1 = (bf16[64,1920]{1,0:T(8,128)(2,1)}, f32[32,8,64]{2,1,0:T(8,128)}) custom-call(bf16[64,1920]{1,0:T(8,128)(2,1)} %get-tuple-element.6.qw_ref, f32[2,8,4,8,128]{4,3,2,1,0:T(8,128)} %get-tuple-element.7.back, s32[32,64]{1,0:T(8,128)} %bitcast.7), custom_call_target="tpu_custom_call" | custom-call | tf_op jit(solution)/shard_map/pick/pallas_call | solution.py:418

commit v4 on v3

--- a/solution.py
+++ b/solution.py
@@ -22,7 +22,7 @@
 HQ = 32
 HL = NDOC * HQ
 BLOCKS = ((0, 512), (512, 512), (1024, 512), (1536, 384))
-PARTS = ((0, 1024), (1024, 896))
+PARTS = ((0, 1920),)
 BF = jnp.bfloat16
 F32 = jnp.float32
 

time: 50.9 us -> 49.6 us (0.974)
  Pallas kernels: 50.1 us -> 48.8 us
    pallas_call x1, Pallas kernels: 47.1 us -> 45.9 us  [body(): pl.pallas_call(kernel, out_shape=(jax.ShapeDtypeStruct((QD, VL), BF), jax...]
where the time goes in v4:
time: 49.6 us; the launch traced here: 49.4 us
  Pallas kernels  48.8 us (98%)
  between operations  0.64 us (1%)
    pallas_call x1, Pallas kernels, body(): pl.pallas_call(kernel, out_shape=(jax.ShapeDtypeStruct((QD, VL), BF), jax...  45.9 us
    pallas_call x1, Pallas kernels, body(): pl.pallas_call(pick, out_shape=(jax.ShapeDtypeStruct((QD, VL), BF), jax.S...  2.92 us

profile of v4, /device:TPU:1, one launch (start us, length us, event | category | flops | bytes accessed | tf_op | source)
XLA Modules:
  0.0 49.4 jit_solution(5440789534024345561)
XLA Ops:
  0.6 45.9 %splade.1 = (bf16[64,1920]{1,0:T(8,128)(2,1)}, f32[2,8,4,8,128]{4,3,2,1,0:T(8,128)}) custom-call(bf16[64,32,768]{2,1,0:T(8,128)(2,1)} %x_hbm.1, s32[32,64]{1,0:T(8,128)} %bitcast.8, bf16[768,768]{1,0:T(8,128)(2,1)} %tw_hbm.1, f32[6,128]{1,0:T(8,128)} %bitcast.10, f32[6,128]{1,0:T(8,128)} %bitcast.11, f32[6,128]{1,0:T(8,128)} %bitcast.12, ...), custom_call_target="tpu_custom_call" | custom-call | tf_op jit(solution)/shard_map/splade/pallas_call | solution.py:366
  46.5 2.9 %pick.1 = (bf16[64,1920]{1,0:T(8,128)(2,1)}, f32[32,8,64]{2,1,0:T(8,128)}) custom-call(bf16[64,1920]{1,0:T(8,128)(2,1)} %get-tuple-element.6.qw_ref, f32[2,8,4,8,128]{4,3,2,1,0:T(8,128)} %get-tuple-element.7.back, s32[32,64]{1,0:T(8,128)} %bitcast.7), custom_call_target="tpu_custom_call" | custom-call | tf_op jit(solution)/shard_map/pick/pallas_call | solution.py:418

commit v5 on v4

--- a/solution.py
+++ b/solution.py
@@ -260,8 +260,9 @@
                 if turn:
                     piece = pltpu.roll(piece, turn, 1)
                 made = jnp.where(lane_group == t, piece, made)
-            pbuf[half, j, 2 * i + axis] = made
-
+            pbuf[half, j, 2 * i + axis] = made.astype(BF)
+
+    occupancy_rows()
     tw_cp.wait()
 
     @pl.loop(0, 4)
@@ -283,7 +284,6 @@
 
     qw_cp = pltpu.make_async_copy(qw_v, qw_ref, osem.at[2])
     qw_cp.start()
-    occupancy_rows()
     pltpu.make_async_copy(dv, dv, dsem).wait()
 
     @pl.loop(0, 2)
@@ -345,7 +345,7 @@
             each = [jnp.broadcast_to(rows[i:i + 1, :], (8, 128)) for i in range(8)]
             accs = [jnp.zeros((8, 128), F32) for _ in range(8)]
             for e in range(NDOC * 4):
-                found = back[half, e // 4, e % 4]
+                found = back[half, e // 4, e % 4].astype(F32)
                 for i in range(8):
                     accs[i] = jnp.where(each[i] == 4 * e, found, accs[i])
             for i in range(8):
@@ -367,7 +367,7 @@
         kernel,
         out_shape=(
             jax.ShapeDtypeStruct((QD, VL), BF),
-            jax.ShapeDtypeStruct((2, NDOC, 4, 8, 128), F32),
+            jax.ShapeDtypeStruct((2, NDOC, 4, 8, 128), BF),
         ),
         in_specs=[any_] * 10,
         out_specs=(any_, any_),
@@ -392,7 +392,7 @@
             pltpu.VMEM((2, 2, 2, 3, 4, 32, HL), BF),
             pltpu.VMEM((2, 2, 2, 4, 32, HL), BF),
             pltpu.VMEM((2, 2, 2, 3, 32, HL), BF),
-            pltpu.VMEM((2, NDOC, 4, 8, 128), F32),
+            pltpu.VMEM((2, NDOC, 4, 8, 128), BF),
             dma((4,)),
             dma((2,)),
             dma(()),

time: 49.6 us -> 49.4 us (level)
  no operation moved by 1% of the time
where the time goes in v5:
time: 49.4 us; the launch traced here: 49.2 us
  Pallas kernels  48.5 us (98%)
  between operations  0.64 us (1%)
    pallas_call x1, Pallas kernels, body(): pl.pallas_call(kernel, out_shape=(jax.ShapeDtypeStruct((QD, VL), BF), jax...  45.6 us
    pallas_call x1, Pallas kernels, body(): pl.pallas_call(pick, out_shape=(jax.ShapeDtypeStruct((QD, VL), BF), jax.S...  2.91 us

profile of v5, /device:TPU:1, one launch (start us, length us, event | category | flops | bytes accessed | tf_op | source)
XLA Modules:
  0.0 49.2 jit_solution(5786293806391773096)
XLA Ops:
  0.6 45.6 %splade.1 = (bf16[64,1920]{1,0:T(8,128)(2,1)}, bf16[2,8,4,8,128]{4,3,2,1,0:T(8,128)(2,1)}) custom-call(bf16[64,32,768]{2,1,0:T(8,128)(2,1)} %x_hbm.1, s32[32,64]{1,0:T(8,128)} %bitcast.8, bf16[768,768]{1,0:T(8,128)(2,1)} %tw_hbm.1, f32[6,128]{1,0:T(8,128)} %bitcast.10, f32[6,128]{1,0:T(8,128)} %bitcast.11, f32[6,128]{1,0:T(8,128)} %bitcast.12, ...), custom_call_target="tpu_custom_call" | custom-call | tf_op jit(solution)/shard_map/splade/pallas_call | solution.py:366
  46.3 2.9 %pick.1 = (bf16[64,1920]{1,0:T(8,128)(2,1)}, f32[32,8,64]{2,1,0:T(8,128)}) custom-call(bf16[64,1920]{1,0:T(8,128)(2,1)} %get-tuple-element.6.qw_ref, bf16[2,8,4,8,128]{4,3,2,1,0:T(8,128)(2,1)} %get-tuple-element.7.back, s32[32,64]{1,0:T(8,128)} %bitcast.7), custom_call_target="tpu_custom_call" | custom-call | tf_op jit(solution)/shard_map/pick/pallas_call | solution.py:418
